TPU v7x, 256 devices: a whole 4x4x8 slice. The times are simulated.
256 devices in a mesh: section: 8 (over z), lon: 32 (over y, x, core).
Axes of the slice: x: 4, y: 4, z: 8, core: 2. Of those that a mesh axis runs over, the one named last changes fastest.
Arguments:
- lanczos_block: bfloat16 [16, 8, 256, 512], P(None, None, 'lon'), may hold values from -9 to 9
- previous: bfloat16 [16, 8, 256, 512], P(None, 'section', 'lon'), may hold values from -6 to 6
- beta_prev: float32 [16, 16], replicated, may hold values from -2 to 2, as said below
- weights: bfloat16 [8, 9, 512, 512], P('section'), may hold values from -0.09375 to 0.09375
- act_slope: bfloat16 [8, 8, 256, 512], P('section', None, 'lon'), may hold values from 0 to 1.09375
- metric: float32 [8, 256], P(None, 'lon'), may hold values from 0.3 to 3
Outputs:
- residual_block: float32 [16, 8, 256, 512], P(None, 'section', 'lon')
- projection: float32 [16, 16], replicated
- residual_gram: float32 [16, 16], replicated
Inputs may be any that keep to these rules, and one draw needn't show every extreme that they name: `beta_prev`: upper triangular, with a positive diagonal.
All inputs are finite; a program needn't handle non-finite values.
Results may differ from a plain program's by a relative error of at most 0.02.
Values may be sent and summed in bfloat16 or wider, within the bound.
No kernel may reach another device: no remote copies, remote signals or barrier semaphores. Data moves between devices by JAX's collectives and lax.ppermute only.
A program may use at most 64 MiB of HBM per device.

v0:
```python
import jax
import jax.numpy as jnp
from jax import lax
from jax.sharding import PartitionSpec as P

K = 16
DILATION_SIZE = 4


def padded(cells, sides, width):
    for axis, dim in sides:
        count = lax.axis_size(axis)
        head = lax.slice_in_dim(cells, 0, width, axis=dim)
        tail = lax.slice_in_dim(cells, cells.shape[dim] - width, cells.shape[dim], axis=dim)
        cells = jnp.concatenate(
            [
                lax.ppermute(tail, axis, [(i, (i + 1) % count) for i in range(count)]),
                cells,
                lax.ppermute(head, axis, [((i + 1) % count, i) for i in range(count)]),
            ],
            axis=dim,
        )
    return cells


def from_behind(shard, axis, by):
    count = lax.axis_size(axis)
    pairs = [(i, i + by) for i in range(count) if 0 <= i + by < count]
    return lax.ppermute(shard, axis, pairs)


def broadcast(shard, axis, root):
    mine = lax.axis_index(axis) == root
    return lax.psum(jnp.where(mine, shard, jnp.zeros_like(shard)), axis)


def spread_taps(input_field, tap_weights, direction_sign, border_width):
    micro_size = input_field.shape[0]
    lat_rows = input_field.shape[1]
    lon_cols = input_field.shape[2] - 2 * border_width
    channels = input_field.shape[3]
    padded_field = jnp.pad(input_field, ((0, 0), (border_width, border_width), (0, 0), (0, 0)))
    summed = jnp.zeros((micro_size * lat_rows * lon_cols, channels), jnp.float32)
    for row_stride in (-1, 0, 1):
        for column_stride in (-1, 0, 1):
            tap_index = 3 * (row_stride + 1) + (column_stride + 1)
            first_row = border_width + direction_sign * row_stride * border_width
            col_start = border_width + direction_sign * column_stride * border_width
            tap_rows = padded_field[
                :, first_row : first_row + lat_rows, col_start : col_start + lon_cols, :
            ].reshape(-1, channels)
            if direction_sign > 0:
                summed = summed + jnp.dot(
                    tap_rows, tap_weights[tap_index], preferred_element_type=jnp.float32
                )
            else:
                summed = summed + lax.dot_general(
                    tap_rows,
                    tap_weights[tap_index],
                    (((1,), (1,)), ((), ())),
                    preferred_element_type=jnp.float32,
                )
    return summed.reshape(micro_size, lat_rows, lon_cols, channels)


def body(lanczos_block, previous, beta_prev, weights, act_slope, metric):
    section_count = lax.axis_size("section")
    section_index = lax.axis_index("section")
    tap_weights = weights[0]
    slope_here = act_slope[0].astype(jnp.float32)[None]
    border_width = DILATION_SIZE
    micro_count = 2
    micro_size = K // micro_count
    slot_shape = (micro_size,) + lanczos_block.shape[1:]
    lon_cols = lanczos_block.shape[2]
    micro_feeds = lanczos_block.reshape((micro_count,) + slot_shape)
    tick_count = micro_count + section_count - 1
    zero_slot = jnp.zeros(slot_shape, jnp.bfloat16)
    empty_store = jnp.zeros((micro_count,) + slot_shape, jnp.bfloat16)

    def forward_layer(rimmed):
        convolved = spread_taps(rimmed, tap_weights, 1, border_width)
        centre = rimmed[:, :, border_width : border_width + lon_cols, :].astype(jnp.float32)
        return (centre + slope_here * convolved).astype(jnp.bfloat16)

    def skip_forward(rimmed):
        return zero_slot

    def forward_tick(state_pair, tick_now):
        inbound, forward_out = state_pair
        micro_index = tick_now - section_index
        active = (micro_index >= 0) & (micro_index < micro_count)
        slot_index = jnp.clip(micro_index, 0, micro_count - 1)
        fed_slot = lax.dynamic_index_in_dim(micro_feeds, slot_index, 0, keepdims=False)
        incoming = jnp.where(section_index == 0, fed_slot, inbound)
        rimmed = padded(incoming, (("lon", 2),), border_width)
        result = lax.cond(active, forward_layer, skip_forward, rimmed)
        keep_slot = active & (section_index == section_count - 1)
        old_slot = lax.dynamic_index_in_dim(forward_out, slot_index, 0, keepdims=False)
        forward_out = lax.dynamic_update_index_in_dim(
            forward_out, jnp.where(keep_slot, result, old_slot), slot_index, 0
        )
        outbound = from_behind(result, "section", 1)
        return ((outbound, forward_out), None)

    (unused_slot, forward_out), unused_out = lax.scan(
        forward_tick, (zero_slot, empty_store), jnp.arange(tick_count, dtype=jnp.int32)
    )
    metric_here = metric[None, :, :, None]

    def backward_layer(operands):
        incoming, rimmed = operands
        convolved = spread_taps(rimmed, tap_weights, -1, border_width)
        return (incoming.astype(jnp.float32) + convolved).astype(jnp.bfloat16)

    def skip_backward(operands):
        return zero_slot

    def backward_tick(state_pair, tick_now):
        inbound, adjoint_out = state_pair
        micro_index = tick_now - (section_count - 1 - section_index)
        active = (micro_index >= 0) & (micro_index < micro_count)
        slot_index = jnp.clip(micro_index, 0, micro_count - 1)
        stored_slot = lax.dynamic_index_in_dim(forward_out, slot_index, 0, keepdims=False)
        started = (metric_here * stored_slot.astype(jnp.float32)).astype(jnp.bfloat16)
        incoming = jnp.where(section_index == section_count - 1, started, inbound)
        sensitivity = (slope_here * incoming.astype(jnp.float32)).astype(jnp.bfloat16)
        rimmed = padded(sensitivity, (("lon", 2),), border_width)
        result = lax.cond(active, backward_layer, skip_backward, (incoming, rimmed))
        keep_slot = active & (section_index == 0)
        old_slot = lax.dynamic_index_in_dim(adjoint_out, slot_index, 0, keepdims=False)
        adjoint_out = lax.dynamic_update_index_in_dim(
            adjoint_out, jnp.where(keep_slot, result, old_slot), slot_index, 0
        )
        outbound = from_behind(result, "section", -1)
        return ((outbound, adjoint_out), None)

    (unused_back, adjoint_out), unused_more = lax.scan(
        backward_tick, (zero_slot, empty_store), jnp.arange(tick_count, dtype=jnp.int32)
    )
    applied = adjoint_out.reshape(lanczos_block.shape)
    applied_all = broadcast(applied, "section", 0)
    row_count = previous.shape[1]
    applied_rows = lax.dynamic_slice_in_dim(applied_all, section_index * row_count, row_count, 1)
    own_block = lax.dynamic_slice_in_dim(lanczos_block, section_index * row_count, row_count, 1)
    high = lax.Precision.HIGHEST
    cell_count = (
        lanczos_block.shape[1]
        * lanczos_block.shape[2]
        * lax.axis_size("lon")
        * lanczos_block.shape[3]
    )
    block_flat = own_block.reshape(K, -1).astype(jnp.float32)
    prev_flat = previous.reshape(K, -1).astype(jnp.float32)
    shifted = applied_rows.reshape(K, -1).astype(jnp.float32) - jnp.dot(
        beta_prev, prev_flat, precision=high
    )
    part_projection = jnp.dot(block_flat, shifted.T, precision=high) / cell_count
    projection = lax.psum(part_projection, ("section", "lon"))
    residual_rows = shifted - jnp.dot(projection.T, block_flat, precision=high)
    part_gram = jnp.dot(residual_rows, residual_rows.T, precision=high) / cell_count
    residual_gram = lax.psum(part_gram, ("section", "lon"))
    return (residual_rows.reshape(own_block.shape), projection, residual_gram)


def solution(mesh):
    return jax.shard_map(
        body,
        mesh=mesh,
        in_specs=(
            P(None, None, "lon", None),
            P(None, "section", "lon", None),
            P(),
            P("section", None, None, None),
            P("section", None, "lon", None),
            P(None, "lon"),
        ),
        out_specs=(P(None, "section", "lon", None), P(), P()),
        check_vma=False,
    )
```

profile of v0, /device:TPU:1, one launch (start us, length us, event | category | flops | bytes accessed | tf_op | source)
XLA Modules:
  0.0 797.1 jit_solution(21797135074578725)
XLA Ops:
  8.3 248.3 %while.27 = (s32[]{:T(128)}, bf16[8,8,8,512]{3,2,1,0:T(8,128)(2,1)S(1)}, bf16[2,8,8,8,512]{4,3,2,1,0:T(8,128)(2,1)S(1)}, s32[9]{0:T(128)S(1)}, s32[]{:T(128)}, /...) while((s32[]{:T(128)}, ...), condition=%wide.region_3.4_spmd, body=%wide.region_0.3_spmd.sunk | while | flops 2422734848 | bytes 67240344 | solution.py:106
  18.7 6.5 conditional.4
  26.8 5.8 collective-permute-done.2
  35.1 8.7 %collective-permute-start = (bf16[8,8,4,512]{3,2,1,0:T(4,128)(2,1)S(1)}, bf16[8,8,4,512]{3,2,1,0:T(4,128)(2,1)S(1)}, u32[]{:S(2)}, u32[]{:S(2)}) collective-permute-start(bf16[8,8,4,512]{3,2,1,0:T(4,128)(2,1)S(1)} %get-tuple-element.424), channel_id=1, source_target_pairs={{1,0},{2,1},{3,2},{4,3},{5,4},{6,5},{7,6},{8,7},{9,8},{10,9},{11,1... | collective-permute-start | bytes 786440 | tf_op jit(solution)/shard_map/while/body/eval_jaxpr/ppermute | solution.py:19
  48.4 6.5 conditional.4
  59.0 5.8 collective-permute-done.2
  67.3 9.0 %collective-permute-start = (bf16[8,8,4,512]{3,2,1,0:T(4,128)(2,1)S(1)}, bf16[8,8,4,512]{3,2,1,0:T(4,128)(2,1)S(1)}, u32[]{:S(2)}, u32[]{:S(2)}) collective-permute-start(bf16[8,8,4,512]{3,2,1,0:T(4,128)(2,1)S(1)} %get-tuple-element.424), channel_id=1, source_target_pairs={{1,0},{2,1},{3,2},{4,3},{5,4},{6,5},{7,6},{8,7},{9,8},{10,9},{11,1... | collective-permute-start | bytes 786440 | tf_op jit(solution)/shard_map/while/body/eval_jaxpr/ppermute | solution.py:19
  80.4 10.6 %collective-permute-start.2 = (bf16[8,8,8,512]{3,2,1,0:T(8,128)(2,1)S(1)}, bf16[8,8,8,512]{3,2,1,0:T(8,128)(2,1)S(1)}, u32[]{:S(2)}, u32[]{:S(2)}) collective-permute-start(bf16[8,8,8,512]{3,2,1,0:T(8,128)(2,1)S(1)} %get-tuple-element.522), channel_id=1, source_target_pairs={{0,32},{32,64},{64,96},{96,128},{128,160},{160,192},{192,224},{1,3... | collective-permute-start | bytes 1572872 | tf_op jit(solution)/shard_map/while/body/eval_jaxpr/ppermute | solution.py:29
  91.2 5.8 collective-permute-done.2
  99.6 8.1 %collective-permute-start = (bf16[8,8,4,512]{3,2,1,0:T(4,128)(2,1)S(1)}, bf16[8,8,4,512]{3,2,1,0:T(4,128)(2,1)S(1)}, u32[]{:S(2)}, u32[]{:S(2)}) collective-permute-start(bf16[8,8,4,512]{3,2,1,0:T(4,128)(2,1)S(1)} %get-tuple-element.424), channel_id=1, source_target_pairs={{1,0},{2,1},{3,2},{4,3},{5,4},{6,5},{7,6},{8,7},{9,8},{10,9},{11,1... | collective-permute-start | bytes 786440 | tf_op jit(solution)/shard_map/while/body/eval_jaxpr/ppermute | solution.py:19
  116.1 5.8 collective-permute-done.2
  124.4 7.2 collective-permute-start
  135.7 8.7 %collective-permute-start.2 = (bf16[8,8,8,512]{3,2,1,0:T(8,128)(2,1)S(1)}, bf16[8,8,8,512]{3,2,1,0:T(8,128)(2,1)S(1)}, u32[]{:S(2)}, u32[]{:S(2)}) collective-permute-start(bf16[8,8,8,512]{3,2,1,0:T(8,128)(2,1)S(1)} %get-tuple-element.522), channel_id=1, source_target_pairs={{0,32},{32,64},{64,96},{96,128},{128,160},{160,192},{192,224},{1,3... | collective-permute-start | bytes 1572872 | tf_op jit(solution)/shard_map/while/body/eval_jaxpr/ppermute | solution.py:29
  144.6 5.8 collective-permute-done.2
  152.9 7.4 collective-permute-start
  168.8 5.8 collective-permute-done.2
  177.1 6.8 collective-permute-start
  188.0 8.7 %collective-permute-start.2 = (bf16[8,8,8,512]{3,2,1,0:T(8,128)(2,1)S(1)}, bf16[8,8,8,512]{3,2,1,0:T(8,128)(2,1)S(1)}, u32[]{:S(2)}, u32[]{:S(2)}) collective-permute-start(bf16[8,8,8,512]{3,2,1,0:T(8,128)(2,1)S(1)} %get-tuple-element.522), channel_id=1, source_target_pairs={{0,32},{32,64},{64,96},{96,128},{128,160},{160,192},{192,224},{1,3... | collective-permute-start | bytes 1572872 | tf_op jit(solution)/shard_map/while/body/eval_jaxpr/ppermute | solution.py:29
  196.9 5.8 collective-permute-done.2
  205.2 6.8 collective-permute-start
  220.5 5.8 collective-permute-done.2
  228.8 6.8 collective-permute-start
  239.7 10.7 %collective-permute-start.2 = (bf16[8,8,8,512]{3,2,1,0:T(8,128)(2,1)S(1)}, bf16[8,8,8,512]{3,2,1,0:T(8,128)(2,1)S(1)}, u32[]{:S(2)}, u32[]{:S(2)}) collective-permute-start(bf16[8,8,8,512]{3,2,1,0:T(8,128)(2,1)S(1)} %get-tuple-element.522), channel_id=1, source_target_pairs={{0,32},{32,64},{64,96},{96,128},{128,160},{160,192},{192,224},{1,3... | collective-permute-start | bytes 1572872 | tf_op jit(solution)/shard_map/while/body/eval_jaxpr/ppermute | solution.py:29
  250.7 5.8 collective-permute-done.2
  257.5 306.7 %while.28 = (s32[]{:T(128)}, bf16[8,8,8,512]{3,2,1,0:T(8,128)(2,1)}, bf16[2,8,8,8,512]{4,3,2,1,0:T(8,128)(2,1)S(1)}, s32[9]{0:T(128)S(1)}, s32[]{:T(128)}, /*ind...) while((s32[]{:T(128)}, ...), condition=%wide.region_7.8_spmd, body=%wide.region_4.7_spmd.sunk | while | flops 2424045568 | bytes 67764888 | solution.py:138
  261.0 6.7 collective-permute-start.3
  274.4 10.3 %collective-permute-done.5 = bf16[8,8,8,512]{3,2,1,0:T(8,128)(2,1)} collective-permute-done((bf16[8,8,8,512]{3,2,1,0:T(8,128)(2,1)S(1)}, bf16[8,8,8,512]{3,2,1,0:T(8,128)(2,1)}, u32[]{:S(2)}, u32[]{:S(2)}) %collective-permute-start.5) | collective-permute-done | bytes 524320 | tf_op jit(solution)/shard_map/while/body/eval_jaxpr/ppermute | solution.py:29
  288.2 6.8 collective-permute-start.3
  301.6 12.0 %collective-permute-done.5 = bf16[8,8,8,512]{3,2,1,0:T(8,128)(2,1)} collective-permute-done((bf16[8,8,8,512]{3,2,1,0:T(8,128)(2,1)S(1)}, bf16[8,8,8,512]{3,2,1,0:T(8,128)(2,1)}, u32[]{:S(2)}, u32[]{:S(2)}) %collective-permute-start.5) | collective-permute-done | bytes 524320 | tf_op jit(solution)/shard_map/while/body/eval_jaxpr/ppermute | solution.py:29
  317.2 6.8 collective-permute-start.3
  330.6 10.5 %collective-permute-done.5 = bf16[8,8,8,512]{3,2,1,0:T(8,128)(2,1)} collective-permute-done((bf16[8,8,8,512]{3,2,1,0:T(8,128)(2,1)S(1)}, bf16[8,8,8,512]{3,2,1,0:T(8,128)(2,1)}, u32[]{:S(2)}, u32[]{:S(2)}) %collective-permute-start.5) | collective-permute-done | bytes 524320 | tf_op jit(solution)/shard_map/while/body/eval_jaxpr/ppermute | solution.py:29
  344.6 6.8 collective-permute-start.3
  358.0 12.0 %collective-permute-done.5 = bf16[8,8,8,512]{3,2,1,0:T(8,128)(2,1)} collective-permute-done((bf16[8,8,8,512]{3,2,1,0:T(8,128)(2,1)S(1)}, bf16[8,8,8,512]{3,2,1,0:T(8,128)(2,1)}, u32[]{:S(2)}, u32[]{:S(2)}) %collective-permute-start.5) | collective-permute-done | bytes 524320 | tf_op jit(solution)/shard_map/while/body/eval_jaxpr/ppermute | solution.py:29
  373.6 6.8 collective-permute-start.3
  386.9 10.0 %collective-permute-done.5 = bf16[8,8,8,512]{3,2,1,0:T(8,128)(2,1)} collective-permute-done((bf16[8,8,8,512]{3,2,1,0:T(8,128)(2,1)S(1)}, bf16[8,8,8,512]{3,2,1,0:T(8,128)(2,1)}, u32[]{:S(2)}, u32[]{:S(2)}) %collective-permute-start.5) | collective-permute-done | bytes 524320 | tf_op jit(solution)/shard_map/while/body/eval_jaxpr/ppermute | solution.py:29
  400.5 6.8 collective-permute-start.3
  413.9 12.5 %collective-permute-done.5 = bf16[8,8,8,512]{3,2,1,0:T(8,128)(2,1)} collective-permute-done((bf16[8,8,8,512]{3,2,1,0:T(8,128)(2,1)S(1)}, bf16[8,8,8,512]{3,2,1,0:T(8,128)(2,1)}, u32[]{:S(2)}, u32[]{:S(2)}) %collective-permute-start.5) | collective-permute-done | bytes 524320 | tf_op jit(solution)/shard_map/while/body/eval_jaxpr/ppermute | solution.py:29
  429.9 6.8 collective-permute-start.3
  443.3 54.9 %collective-permute-done.5 = bf16[8,8,8,512]{3,2,1,0:T(8,128)(2,1)} collective-permute-done((bf16[8,8,8,512]{3,2,1,0:T(8,128)(2,1)S(1)}, bf16[8,8,8,512]{3,2,1,0:T(8,128)(2,1)}, u32[]{:S(2)}, u32[]{:S(2)}) %collective-permute-start.5) | collective-permute-done | bytes 524320 | tf_op jit(solution)/shard_map/while/body/eval_jaxpr/ppermute | solution.py:29
  501.8 6.8 collective-permute-start.3
  513.6 6.8 conditional.5
  522.0 10.0 %collective-permute-done.5 = bf16[8,8,8,512]{3,2,1,0:T(8,128)(2,1)} collective-permute-done((bf16[8,8,8,512]{3,2,1,0:T(8,128)(2,1)S(1)}, bf16[8,8,8,512]{3,2,1,0:T(8,128)(2,1)}, u32[]{:S(2)}, u32[]{:S(2)}) %collective-permute-start.5) | collective-permute-done | bytes 524320 | tf_op jit(solution)/shard_map/while/body/eval_jaxpr/ppermute | solution.py:29
  535.5 6.8 collective-permute-start.3
  547.3 6.8 conditional.5
  555.7 8.5 %collective-permute-done.5 = bf16[8,8,8,512]{3,2,1,0:T(8,128)(2,1)} collective-permute-done((bf16[8,8,8,512]{3,2,1,0:T(8,128)(2,1)S(1)}, bf16[8,8,8,512]{3,2,1,0:T(8,128)(2,1)}, u32[]{:S(2)}, u32[]{:S(2)}) %collective-permute-start.5) | collective-permute-done | bytes 524320 | tf_op jit(solution)/shard_map/while/body/eval_jaxpr/ppermute | solution.py:29
  566.4 67.9 %all-reduce.4.cloned.1.call-done = bf16[16,8,8,512]{3,2,0,1:T(8,128)(2,1)} async-done(((bf16[16,8,8,512]{3,2,0,1:T(8,128)(2,1)}), bf16[16,8,8,512]{3,2,0,1:T(8,128)(2,1)}) %all-reduce.4.cloned.1.call-update) | async-done | bytes 1048592 | tf_op jit(solution)/shard_map/psum | solution.py:34
  636.0 79.2 %psum.22 = f32[16,16]{1,0:T(8,128)S(1)} all-reduce(f32[16,16]{1,0:T(8,128)S(1)} %convolution_multiply_fusion.1), channel_id=1, replica_groups=mesh['section'=8,'lon'=32] {'section','lon'}, use_global_device_ids=true, to_apply=%region_9.10 | all-reduce | flops 256 | bytes 2048 | tf_op jit(solution)/shard_map/psum | solution.py:159
  716.9 73.3 %psum.23 = f32[16,16]{1,0:T(8,128)} all-reduce(f32[16,16]{1,0:T(8,128)S(1)} %convolution_multiply_fusion), channel_id=1, replica_groups=mesh['section'=8,'lon'=32] {'section','lon'}, use_global_device_ids=true, to_apply=%region_10.11 | all-reduce | flops 256 | bytes 2048 | tf_op jit(solution)/shard_map/psum | solution.py:162
  (286 shorter events, 196.7 us)
Async XLA Ops:
  7.2 627.2 %all-reduce.4.cloned.1.call-start = ((), (), s32[]{:S(2)}) async-start(), calls=%async_computation | async-start | bytes 2097152 | tf_op jit(solution)/shard_map/psum | solution.py:34
  10.8 6.7 collective-permute-start
  14.0 4.0 collective-permute-start.1
  25.2 7.4 collective-permute-start.2
  35.1 11.0 %collective-permute-start = (bf16[8,8,4,512]{3,2,1,0:T(4,128)(2,1)S(1)}, bf16[8,8,4,512]{3,2,1,0:T(4,128)(2,1)S(1)}, u32[]{:S(2)}, u32[]{:S(2)}) collective-permute-start(bf16[8,8,4,512]{3,2,1,0:T(4,128)(2,1)S(1)} %get-tuple-element.424), channel_id=1, source_target_pairs={{1,0},{2,1},{3,2},{4,3},{5,4},{6,5},{7,6},{8,7},{9,8},{10,9},{11,1... | collective-permute-start | bytes 786440 | tf_op jit(solution)/shard_map/while/body/eval_jaxpr/ppermute | solution.py:19
  43.8 3.9 collective-permute-start.1
  54.9 9.9 %collective-permute-start.2 = (bf16[8,8,8,512]{3,2,1,0:T(8,128)(2,1)S(1)}, bf16[8,8,8,512]{3,2,1,0:T(8,128)(2,1)S(1)}, u32[]{:S(2)}, u32[]{:S(2)}) collective-permute-start(bf16[8,8,8,512]{3,2,1,0:T(8,128)(2,1)S(1)} %get-tuple-element.522), channel_id=1, source_target_pairs={{0,32},{32,64},{64,96},{96,128},{128,160},{160,192},{192,224},{1,3... | collective-permute-start | bytes 1572872 | tf_op jit(solution)/shard_map/while/body/eval_jaxpr/ppermute | solution.py:29
  67.3 10.2 %collective-permute-start = (bf16[8,8,4,512]{3,2,1,0:T(4,128)(2,1)S(1)}, bf16[8,8,4,512]{3,2,1,0:T(4,128)(2,1)S(1)}, u32[]{:S(2)}, u32[]{:S(2)}) collective-permute-start(bf16[8,8,4,512]{3,2,1,0:T(4,128)(2,1)S(1)} %get-tuple-element.424), channel_id=1, source_target_pairs={{1,0},{2,1},{3,2},{4,3},{5,4},{6,5},{7,6},{8,7},{9,8},{10,9},{11,1... | collective-permute-start | bytes 786440 | tf_op jit(solution)/shard_map/while/body/eval_jaxpr/ppermute | solution.py:19
  76.3 3.3 collective-permute-start.1
  80.4 16.7 %collective-permute-start.2 = (bf16[8,8,8,512]{3,2,1,0:T(8,128)(2,1)S(1)}, bf16[8,8,8,512]{3,2,1,0:T(8,128)(2,1)S(1)}, u32[]{:S(2)}, u32[]{:S(2)}) collective-permute-start(bf16[8,8,8,512]{3,2,1,0:T(8,128)(2,1)S(1)} %get-tuple-element.522), channel_id=1, source_target_pairs={{0,32},{32,64},{64,96},{96,128},{128,160},{160,192},{192,224},{1,3... | collective-permute-start | bytes 1572872 | tf_op jit(solution)/shard_map/while/body/eval_jaxpr/ppermute | solution.py:29
  99.6 9.3 %collective-permute-start = (bf16[8,8,4,512]{3,2,1,0:T(4,128)(2,1)S(1)}, bf16[8,8,4,512]{3,2,1,0:T(4,128)(2,1)S(1)}, u32[]{:S(2)}, u32[]{:S(2)}) collective-permute-start(bf16[8,8,4,512]{3,2,1,0:T(4,128)(2,1)S(1)} %get-tuple-element.424), channel_id=1, source_target_pairs={{1,0},{2,1},{3,2},{4,3},{5,4},{6,5},{7,6},{8,7},{9,8},{10,9},{11,1... | collective-permute-start | bytes 786440 | tf_op jit(solution)/shard_map/while/body/eval_jaxpr/ppermute | solution.py:19
  107.7 3.3 collective-permute-start.1
  111.7 10.2 %collective-permute-start.2 = (bf16[8,8,8,512]{3,2,1,0:T(8,128)(2,1)S(1)}, bf16[8,8,8,512]{3,2,1,0:T(8,128)(2,1)S(1)}, u32[]{:S(2)}, u32[]{:S(2)}) collective-permute-start(bf16[8,8,8,512]{3,2,1,0:T(8,128)(2,1)S(1)} %get-tuple-element.522), channel_id=1, source_target_pairs={{0,32},{32,64},{64,96},{96,128},{128,160},{160,192},{192,224},{1,3... | collective-permute-start | bytes 1572872 | tf_op jit(solution)/shard_map/while/body/eval_jaxpr/ppermute | solution.py:29
  124.4 8.3 %collective-permute-start = (bf16[8,8,4,512]{3,2,1,0:T(4,128)(2,1)S(1)}, bf16[8,8,4,512]{3,2,1,0:T(4,128)(2,1)S(1)}, u32[]{:S(2)}, u32[]{:S(2)}) collective-permute-start(bf16[8,8,4,512]{3,2,1,0:T(4,128)(2,1)S(1)} %get-tuple-element.424), channel_id=1, source_target_pairs={{1,0},{2,1},{3,2},{4,3},{5,4},{6,5},{7,6},{8,7},{9,8},{10,9},{11,1... | collective-permute-start | bytes 786440 | tf_op jit(solution)/shard_map/while/body/eval_jaxpr/ppermute | solution.py:19
  131.6 3.3 collective-permute-start.1
  135.7 14.8 %collective-permute-start.2 = (bf16[8,8,8,512]{3,2,1,0:T(8,128)(2,1)S(1)}, bf16[8,8,8,512]{3,2,1,0:T(8,128)(2,1)S(1)}, u32[]{:S(2)}, u32[]{:S(2)}) collective-permute-start(bf16[8,8,8,512]{3,2,1,0:T(8,128)(2,1)S(1)} %get-tuple-element.522), channel_id=1, source_target_pairs={{0,32},{32,64},{64,96},{96,128},{128,160},{160,192},{192,224},{1,3... | collective-permute-start | bytes 1572872 | tf_op jit(solution)/shard_map/while/body/eval_jaxpr/ppermute | solution.py:29
  152.9 8.6 %collective-permute-start = (bf16[8,8,4,512]{3,2,1,0:T(4,128)(2,1)S(1)}, bf16[8,8,4,512]{3,2,1,0:T(4,128)(2,1)S(1)}, u32[]{:S(2)}, u32[]{:S(2)}) collective-permute-start(bf16[8,8,4,512]{3,2,1,0:T(4,128)(2,1)S(1)} %get-tuple-element.424), channel_id=1, source_target_pairs={{1,0},{2,1},{3,2},{4,3},{5,4},{6,5},{7,6},{8,7},{9,8},{10,9},{11,1... | collective-permute-start | bytes 786440 | tf_op jit(solution)/shard_map/while/body/eval_jaxpr/ppermute | solution.py:19
  160.3 3.3 collective-permute-start.1
  164.4 10.2 %collective-permute-start.2 = (bf16[8,8,8,512]{3,2,1,0:T(8,128)(2,1)S(1)}, bf16[8,8,8,512]{3,2,1,0:T(8,128)(2,1)S(1)}, u32[]{:S(2)}, u32[]{:S(2)}) collective-permute-start(bf16[8,8,8,512]{3,2,1,0:T(8,128)(2,1)S(1)} %get-tuple-element.522), channel_id=1, source_target_pairs={{0,32},{32,64},{64,96},{96,128},{128,160},{160,192},{192,224},{1,3... | collective-permute-start | bytes 1572872 | tf_op jit(solution)/shard_map/while/body/eval_jaxpr/ppermute | solution.py:29
  177.1 8.0 %collective-permute-start = (bf16[8,8,4,512]{3,2,1,0:T(4,128)(2,1)S(1)}, bf16[8,8,4,512]{3,2,1,0:T(4,128)(2,1)S(1)}, u32[]{:S(2)}, u32[]{:S(2)}) collective-permute-start(bf16[8,8,4,512]{3,2,1,0:T(4,128)(2,1)S(1)} %get-tuple-element.424), channel_id=1, source_target_pairs={{1,0},{2,1},{3,2},{4,3},{5,4},{6,5},{7,6},{8,7},{9,8},{10,9},{11,1... | collective-permute-start | bytes 786440 | tf_op jit(solution)/shard_map/while/body/eval_jaxpr/ppermute | solution.py:19
  183.9 3.3 collective-permute-start.1
  188.0 14.8 %collective-permute-start.2 = (bf16[8,8,8,512]{3,2,1,0:T(8,128)(2,1)S(1)}, bf16[8,8,8,512]{3,2,1,0:T(8,128)(2,1)S(1)}, u32[]{:S(2)}, u32[]{:S(2)}) collective-permute-start(bf16[8,8,8,512]{3,2,1,0:T(8,128)(2,1)S(1)} %get-tuple-element.522), channel_id=1, source_target_pairs={{0,32},{32,64},{64,96},{96,128},{128,160},{160,192},{192,224},{1,3... | collective-permute-start | bytes 1572872 | tf_op jit(solution)/shard_map/while/body/eval_jaxpr/ppermute | solution.py:29
  205.2 8.0 %collective-permute-start = (bf16[8,8,4,512]{3,2,1,0:T(4,128)(2,1)S(1)}, bf16[8,8,4,512]{3,2,1,0:T(4,128)(2,1)S(1)}, u32[]{:S(2)}, u32[]{:S(2)}) collective-permute-start(bf16[8,8,4,512]{3,2,1,0:T(4,128)(2,1)S(1)} %get-tuple-element.424), channel_id=1, source_target_pairs={{1,0},{2,1},{3,2},{4,3},{5,4},{6,5},{7,6},{8,7},{9,8},{10,9},{11,1... | collective-permute-start | bytes 786440 | tf_op jit(solution)/shard_map/while/body/eval_jaxpr/ppermute | solution.py:19
  212.0 3.3 collective-permute-start.1
  216.1 10.2 %collective-permute-start.2 = (bf16[8,8,8,512]{3,2,1,0:T(8,128)(2,1)S(1)}, bf16[8,8,8,512]{3,2,1,0:T(8,128)(2,1)S(1)}, u32[]{:S(2)}, u32[]{:S(2)}) collective-permute-start(bf16[8,8,8,512]{3,2,1,0:T(8,128)(2,1)S(1)} %get-tuple-element.522), channel_id=1, source_target_pairs={{0,32},{32,64},{64,96},{96,128},{128,160},{160,192},{192,224},{1,3... | collective-permute-start | bytes 1572872 | tf_op jit(solution)/shard_map/while/body/eval_jaxpr/ppermute | solution.py:29
  228.8 8.0 %collective-permute-start = (bf16[8,8,4,512]{3,2,1,0:T(4,128)(2,1)S(1)}, bf16[8,8,4,512]{3,2,1,0:T(4,128)(2,1)S(1)}, u32[]{:S(2)}, u32[]{:S(2)}) collective-permute-start(bf16[8,8,4,512]{3,2,1,0:T(4,128)(2,1)S(1)} %get-tuple-element.424), channel_id=1, source_target_pairs={{1,0},{2,1},{3,2},{4,3},{5,4},{6,5},{7,6},{8,7},{9,8},{10,9},{11,1... | collective-permute-start | bytes 786440 | tf_op jit(solution)/shard_map/while/body/eval_jaxpr/ppermute | solution.py:19
  235.6 3.3 collective-permute-start.1
  239.7 16.8 %collective-permute-start.2 = (bf16[8,8,8,512]{3,2,1,0:T(8,128)(2,1)S(1)}, bf16[8,8,8,512]{3,2,1,0:T(8,128)(2,1)S(1)}, u32[]{:S(2)}, u32[]{:S(2)}) collective-permute-start(bf16[8,8,8,512]{3,2,1,0:T(8,128)(2,1)S(1)} %get-tuple-element.522), channel_id=1, source_target_pairs={{0,32},{32,64},{64,96},{96,128},{128,160},{160,192},{192,224},{1,3... | collective-permute-start | bytes 1572872 | tf_op jit(solution)/shard_map/while/body/eval_jaxpr/ppermute | solution.py:29
  261.0 8.2 %collective-permute-start.3 = (bf16[8,8,4,512]{3,2,1,0:T(4,128)(2,1)}, bf16[8,8,4,512]{3,2,1,0:T(4,128)(2,1)}, u32[]{:S(2)}, u32[]{:S(2)}) collective-permute-start(bf16[8,8,4,512]{3,2,1,0:T(4,128)(2,1)} %get-tuple-element.439), channel_id=1, source_target_pairs={{1,0},{2,1},{3,2},{4,3},{5,4},{6,5},{7,6},{8,7},{9,8},{10,9},{11,1... | collective-permute-start | bytes 786440 | tf_op jit(solution)/shard_map/while/body/eval_jaxpr/ppermute | solution.py:19
  267.8 3.3 collective-permute-start.4
  272.8 11.8 %collective-permute-start.5 = (bf16[8,8,8,512]{3,2,1,0:T(8,128)(2,1)S(1)}, bf16[8,8,8,512]{3,2,1,0:T(8,128)(2,1)}, u32[]{:S(2)}, u32[]{:S(2)}) collective-permute-start(bf16[8,8,8,512]{3,2,1,0:T(8,128)(2,1)S(1)} %get-tuple-element.523), channel_id=1, source_target_pairs={{32,0},{64,32},{96,64},{128,96},{160,128},{192,160},{224,192},{33,... | collective-permute-start | bytes 1572872 | tf_op jit(solution)/shard_map/while/body/eval_jaxpr/ppermute | solution.py:29
  288.2 8.3 %collective-permute-start.3 = (bf16[8,8,4,512]{3,2,1,0:T(4,128)(2,1)}, bf16[8,8,4,512]{3,2,1,0:T(4,128)(2,1)}, u32[]{:S(2)}, u32[]{:S(2)}) collective-permute-start(bf16[8,8,4,512]{3,2,1,0:T(4,128)(2,1)} %get-tuple-element.439), channel_id=1, source_target_pairs={{1,0},{2,1},{3,2},{4,3},{5,4},{6,5},{7,6},{8,7},{9,8},{10,9},{11,1... | collective-permute-start | bytes 786440 | tf_op jit(solution)/shard_map/while/body/eval_jaxpr/ppermute | solution.py:19
  295.0 3.3 collective-permute-start.4
  300.1 13.6 %collective-permute-start.5 = (bf16[8,8,8,512]{3,2,1,0:T(8,128)(2,1)S(1)}, bf16[8,8,8,512]{3,2,1,0:T(8,128)(2,1)}, u32[]{:S(2)}, u32[]{:S(2)}) collective-permute-start(bf16[8,8,8,512]{3,2,1,0:T(8,128)(2,1)S(1)} %get-tuple-element.523), channel_id=1, source_target_pairs={{32,0},{64,32},{96,64},{128,96},{160,128},{192,160},{224,192},{33,... | collective-permute-start | bytes 1572872 | tf_op jit(solution)/shard_map/while/body/eval_jaxpr/ppermute | solution.py:29
  317.2 8.3 %collective-permute-start.3 = (bf16[8,8,4,512]{3,2,1,0:T(4,128)(2,1)}, bf16[8,8,4,512]{3,2,1,0:T(4,128)(2,1)}, u32[]{:S(2)}, u32[]{:S(2)}) collective-permute-start(bf16[8,8,4,512]{3,2,1,0:T(4,128)(2,1)} %get-tuple-element.439), channel_id=1, source_target_pairs={{1,0},{2,1},{3,2},{4,3},{5,4},{6,5},{7,6},{8,7},{9,8},{10,9},{11,1... | collective-permute-start | bytes 786440 | tf_op jit(solution)/shard_map/while/body/eval_jaxpr/ppermute | solution.py:19
  329.0 12.0 %collective-permute-start.5 = (bf16[8,8,8,512]{3,2,1,0:T(8,128)(2,1)S(1)}, bf16[8,8,8,512]{3,2,1,0:T(8,128)(2,1)}, u32[]{:S(2)}, u32[]{:S(2)}) collective-permute-start(bf16[8,8,8,512]{3,2,1,0:T(8,128)(2,1)S(1)} %get-tuple-element.523), channel_id=1, source_target_pairs={{32,0},{64,32},{96,64},{128,96},{160,128},{192,160},{224,192},{33,... | collective-permute-start | bytes 1572872 | tf_op jit(solution)/shard_map/while/body/eval_jaxpr/ppermute | solution.py:29
  344.6 8.3 %collective-permute-start.3 = (bf16[8,8,4,512]{3,2,1,0:T(4,128)(2,1)}, bf16[8,8,4,512]{3,2,1,0:T(4,128)(2,1)}, u32[]{:S(2)}, u32[]{:S(2)}) collective-permute-start(bf16[8,8,4,512]{3,2,1,0:T(4,128)(2,1)} %get-tuple-element.439), channel_id=1, source_target_pairs={{1,0},{2,1},{3,2},{4,3},{5,4},{6,5},{7,6},{8,7},{9,8},{10,9},{11,1... | collective-permute-start | bytes 786440 | tf_op jit(solution)/shard_map/while/body/eval_jaxpr/ppermute | solution.py:19
  356.4 13.6 %collective-permute-start.5 = (bf16[8,8,8,512]{3,2,1,0:T(8,128)(2,1)S(1)}, bf16[8,8,8,512]{3,2,1,0:T(8,128)(2,1)}, u32[]{:S(2)}, u32[]{:S(2)}) collective-permute-start(bf16[8,8,8,512]{3,2,1,0:T(8,128)(2,1)S(1)} %get-tuple-element.523), channel_id=1, source_target_pairs={{32,0},{64,32},{96,64},{128,96},{160,128},{192,160},{224,192},{33,... | collective-permute-start | bytes 1572872 | tf_op jit(solution)/shard_map/while/body/eval_jaxpr/ppermute | solution.py:29
  373.6 8.3 %collective-permute-start.3 = (bf16[8,8,4,512]{3,2,1,0:T(4,128)(2,1)}, bf16[8,8,4,512]{3,2,1,0:T(4,128)(2,1)}, u32[]{:S(2)}, u32[]{:S(2)}) collective-permute-start(bf16[8,8,4,512]{3,2,1,0:T(4,128)(2,1)} %get-tuple-element.439), channel_id=1, source_target_pairs={{1,0},{2,1},{3,2},{4,3},{5,4},{6,5},{7,6},{8,7},{9,8},{10,9},{11,1... | collective-permute-start | bytes 786440 | tf_op jit(solution)/shard_map/while/body/eval_jaxpr/ppermute | solution.py:19
  385.4 11.5 %collective-permute-start.5 = (bf16[8,8,8,512]{3,2,1,0:T(8,128)(2,1)S(1)}, bf16[8,8,8,512]{3,2,1,0:T(8,128)(2,1)}, u32[]{:S(2)}, u32[]{:S(2)}) collective-permute-start(bf16[8,8,8,512]{3,2,1,0:T(8,128)(2,1)S(1)} %get-tuple-element.523), channel_id=1, source_target_pairs={{32,0},{64,32},{96,64},{128,96},{160,128},{192,160},{224,192},{33,... | collective-permute-start | bytes 1572872 | tf_op jit(solution)/shard_map/while/body/eval_jaxpr/ppermute | solution.py:29
  400.5 8.3 %collective-permute-start.3 = (bf16[8,8,4,512]{3,2,1,0:T(4,128)(2,1)}, bf16[8,8,4,512]{3,2,1,0:T(4,128)(2,1)}, u32[]{:S(2)}, u32[]{:S(2)}) collective-permute-start(bf16[8,8,4,512]{3,2,1,0:T(4,128)(2,1)} %get-tuple-element.439), channel_id=1, source_target_pairs={{1,0},{2,1},{3,2},{4,3},{5,4},{6,5},{7,6},{8,7},{9,8},{10,9},{11,1... | collective-permute-start | bytes 786440 | tf_op jit(solution)/shard_map/while/body/eval_jaxpr/ppermute | solution.py:19
  412.4 14.0 %collective-permute-start.5 = (bf16[8,8,8,512]{3,2,1,0:T(8,128)(2,1)S(1)}, bf16[8,8,8,512]{3,2,1,0:T(8,128)(2,1)}, u32[]{:S(2)}, u32[]{:S(2)}) collective-permute-start(bf16[8,8,8,512]{3,2,1,0:T(8,128)(2,1)S(1)} %get-tuple-element.523), channel_id=1, source_target_pairs={{32,0},{64,32},{96,64},{128,96},{160,128},{192,160},{224,192},{33,... | collective-permute-start | bytes 1572872 | tf_op jit(solution)/shard_map/while/body/eval_jaxpr/ppermute | solution.py:29
  429.9 8.3 %collective-permute-start.3 = (bf16[8,8,4,512]{3,2,1,0:T(4,128)(2,1)}, bf16[8,8,4,512]{3,2,1,0:T(4,128)(2,1)}, u32[]{:S(2)}, u32[]{:S(2)}) collective-permute-start(bf16[8,8,4,512]{3,2,1,0:T(4,128)(2,1)} %get-tuple-element.439), channel_id=1, source_target_pairs={{1,0},{2,1},{3,2},{4,3},{5,4},{6,5},{7,6},{8,7},{9,8},{10,9},{11,1... | collective-permute-start | bytes 786440 | tf_op jit(solution)/shard_map/while/body/eval_jaxpr/ppermute | solution.py:19
  441.8 56.5 %collective-permute-start.5 = (bf16[8,8,8,512]{3,2,1,0:T(8,128)(2,1)S(1)}, bf16[8,8,8,512]{3,2,1,0:T(8,128)(2,1)}, u32[]{:S(2)}, u32[]{:S(2)}) collective-permute-start(bf16[8,8,8,512]{3,2,1,0:T(8,128)(2,1)S(1)} %get-tuple-element.523), channel_id=1, source_target_pairs={{32,0},{64,32},{96,64},{128,96},{160,128},{192,160},{224,192},{33,... | collective-permute-start | bytes 1572872 | tf_op jit(solution)/shard_map/while/body/eval_jaxpr/ppermute | solution.py:29
  501.8 8.3 %collective-permute-start.3 = (bf16[8,8,4,512]{3,2,1,0:T(4,128)(2,1)}, bf16[8,8,4,512]{3,2,1,0:T(4,128)(2,1)}, u32[]{:S(2)}, u32[]{:S(2)}) collective-permute-start(bf16[8,8,4,512]{3,2,1,0:T(4,128)(2,1)} %get-tuple-element.439), channel_id=1, source_target_pairs={{1,0},{2,1},{3,2},{4,3},{5,4},{6,5},{7,6},{8,7},{9,8},{10,9},{11,1... | collective-permute-start | bytes 786440 | tf_op jit(solution)/shard_map/while/body/eval_jaxpr/ppermute | solution.py:19
  520.4 11.5 %collective-permute-start.5 = (bf16[8,8,8,512]{3,2,1,0:T(8,128)(2,1)S(1)}, bf16[8,8,8,512]{3,2,1,0:T(8,128)(2,1)}, u32[]{:S(2)}, u32[]{:S(2)}) collective-permute-start(bf16[8,8,8,512]{3,2,1,0:T(8,128)(2,1)S(1)} %get-tuple-element.523), channel_id=1, source_target_pairs={{32,0},{64,32},{96,64},{128,96},{160,128},{192,160},{224,192},{33,... | collective-permute-start | bytes 1572872 | tf_op jit(solution)/shard_map/while/body/eval_jaxpr/ppermute | solution.py:29
  535.5 8.3 %collective-permute-start.3 = (bf16[8,8,4,512]{3,2,1,0:T(4,128)(2,1)}, bf16[8,8,4,512]{3,2,1,0:T(4,128)(2,1)}, u32[]{:S(2)}, u32[]{:S(2)}) collective-permute-start(bf16[8,8,4,512]{3,2,1,0:T(4,128)(2,1)} %get-tuple-element.439), channel_id=1, source_target_pairs={{1,0},{2,1},{3,2},{4,3},{5,4},{6,5},{7,6},{8,7},{9,8},{10,9},{11,1... | collective-permute-start | bytes 786440 | tf_op jit(solution)/shard_map/while/body/eval_jaxpr/ppermute | solution.py:19
  554.2 10.0 %collective-permute-start.5 = (bf16[8,8,8,512]{3,2,1,0:T(8,128)(2,1)S(1)}, bf16[8,8,8,512]{3,2,1,0:T(8,128)(2,1)}, u32[]{:S(2)}, u32[]{:S(2)}) collective-permute-start(bf16[8,8,8,512]{3,2,1,0:T(8,128)(2,1)S(1)} %get-tuple-element.523), channel_id=1, source_target_pairs={{32,0},{64,32},{96,64},{128,96},{160,128},{192,160},{224,192},{33,... | collective-permute-start | bytes 1572872 | tf_op jit(solution)/shard_map/while/body/eval_jaxpr/ppermute | solution.py:29
  (15 other events, 986.3 us)
Sparse Core Ops, SparseCore 0:
  565.5 68.8 all-reduce.3
where the time goes:
time: 799 us; the launch traced here: 797 us
  waiting for transfers between devices  322 us (40%)
  starting transfers between devices  193 us (24%)
  blocking collectives  153 us (19%)
  other arithmetic  49.3 us (6%)
  local copies, waits for them, and re-layouts  35.4 us (4%)
  matrix products  17.6 us (2%)
  between operations  14.2 us (2%)
  loops' own time  12.5 us (2%)
    ppermute x18, waiting for transfers between devices, from_behind(): return lax.ppermute(shard, axis, pairs)  193 us
    ppermute x18, starting transfers between devices, padded(): lax.ppermute(head, axis, [((i + 1) % count, i) for i in range(count)])  125 us
    psum x1, blocking collectives, body(): projection = lax.psum(part_projection, ('section', 'lon'))  79.2 us
    psum x1, blocking collectives, body(): residual_gram = lax.psum(part_gram, ('section', 'lon'))  73.3 us
    psum x1, waiting for transfers between devices, broadcast(): return lax.psum(jnp.where(mine, shard, jnp.zeros_like(shard)), axis)  67.9 us
    ppermute x18, starting transfers between devices, from_behind(): return lax.ppermute(shard, axis, pairs)  67.9 us
    ppermute x18, waiting for transfers between devices, padded(): lax.ppermute(tail, axis, [(i, (i + 1) % count) for i in range(count)])  33.5 us
    ppermute x18, waiting for transfers between devices, padded(): lax.ppermute(head, axis, [((i + 1) % count, i) for i in range(count)])  27.4 us
  transfers between devices with their start and end apart: 55, of which 55 were waited for; matrix products, arithmetic and copies ran while one was open for 1% of the time, Pallas kernels for 0%

commit v1 on v0

--- a/solution.py
+++ b/solution.py
@@ -156,7 +156,8 @@
         beta_prev, prev_flat, precision=high
     )
     part_projection = jnp.dot(block_flat, shifted.T, precision=high) / cell_count
-    projection = lax.psum(part_projection, ("section", "lon"))
+    partial = lax.psum(part_projection, "lon")
+    projection = lax.psum(partial, "section")
     residual_rows = shifted - jnp.dot(projection.T, block_flat, precision=high)
     part_gram = jnp.dot(residual_rows, residual_rows.T, precision=high) / cell_count
     residual_gram = lax.psum(part_gram, ("section", "lon"))

time: 799 us -> 804 us (level)
    psum x1 -> x2, blocking collectives: 79.2 us -> 81.2 us  [the longest x1 68.1 us: body(): partial = lax.psum(part_projection, 'lon')]
where the time goes in v1:
time: 804 us; the launch traced here: 802 us
  waiting for transfers between devices  322 us (40%)
  starting transfers between devices  193 us (24%)
  blocking collectives  156 us (19%)
  other arithmetic  49.3 us (6%)
  local copies, waits for them, and re-layouts  36 us (4%)
  matrix products  17.6 us (2%)
  between operations  14.2 us (2%)
  loops' own time  13.3 us (2%)
    ppermute x18, waiting for transfers between devices, from_behind(): return lax.ppermute(shard, axis, pairs)  193 us
    ppermute x18, starting transfers between devices, padded(): lax.ppermute(head, axis, [((i + 1) % count, i) for i in range(count)])  125 us
    psum x1, blocking collectives, body(): residual_gram = lax.psum(part_gram, ('section', 'lon'))  74.7 us
    psum x1, blocking collectives, body(): partial = lax.psum(part_projection, 'lon')  68.1 us
    ppermute x18, starting transfers between devices, from_behind(): return lax.ppermute(shard, axis, pairs)  67.9 us
    psum x1, waiting for transfers between devices, broadcast(): return lax.psum(jnp.where(mine, shard, jnp.zeros_like(shard)), axis)  67.9 us
    ppermute x18, waiting for transfers between devices, padded(): lax.ppermute(tail, axis, [(i, (i + 1) % count) for i in range(count)])  33.5 us
    ppermute x18, waiting for transfers between devices, padded(): lax.ppermute(head, axis, [((i + 1) % count, i) for i in range(count)])  27.4 us
  transfers between devices with their start and end apart: 55, of which 55 were waited for; matrix products, arithmetic and copies ran while one was open for 1% of the time, Pallas kernels for 0%

profile of v1, /device:TPU:1, one launch (start us, length us, event | category | flops | bytes accessed | tf_op | source)
XLA Modules:
  0.0 801.7 jit_solution(9775872552224720644)
XLA Ops:
  8.3 249.6 %while.27 = (s32[]{:T(128)}, bf16[8,8,8,512]{3,2,1,0:T(8,128)(2,1)S(1)}, bf16[2,8,8,8,512]{4,3,2,1,0:T(8,128)(2,1)S(1)}, s32[9]{0:T(128)S(1)}, s32[]{:T(128)}, /...) while((s32[]{:T(128)}, ...), condition=%wide.region_3.4_spmd, body=%wide.region_0.3_spmd.sunk | while | flops 2422734848 | bytes 67240344 | solution.py:106
  18.8 6.5 conditional.4
  26.9 5.8 collective-permute-done.2
  35.4 8.7 %collective-permute-start = (bf16[8,8,4,512]{3,2,1,0:T(4,128)(2,1)S(1)}, bf16[8,8,4,512]{3,2,1,0:T(4,128)(2,1)S(1)}, u32[]{:S(2)}, u32[]{:S(2)}) collective-permute-start(bf16[8,8,4,512]{3,2,1,0:T(4,128)(2,1)S(1)} %get-tuple-element.424), channel_id=1, source_target_pairs={{1,0},{2,1},{3,2},{4,3},{5,4},{6,5},{7,6},{8,7},{9,8},{10,9},{11,1... | collective-permute-start | bytes 786440 | tf_op jit(solution)/shard_map/while/body/eval_jaxpr/ppermute | solution.py:19
  48.7 6.5 conditional.4
  59.3 5.8 collective-permute-done.2
  67.8 9.0 %collective-permute-start = (bf16[8,8,4,512]{3,2,1,0:T(4,128)(2,1)S(1)}, bf16[8,8,4,512]{3,2,1,0:T(4,128)(2,1)S(1)}, u32[]{:S(2)}, u32[]{:S(2)}) collective-permute-start(bf16[8,8,4,512]{3,2,1,0:T(4,128)(2,1)S(1)} %get-tuple-element.424), channel_id=1, source_target_pairs={{1,0},{2,1},{3,2},{4,3},{5,4},{6,5},{7,6},{8,7},{9,8},{10,9},{11,1... | collective-permute-start | bytes 786440 | tf_op jit(solution)/shard_map/while/body/eval_jaxpr/ppermute | solution.py:19
  80.9 10.6 %collective-permute-start.2 = (bf16[8,8,8,512]{3,2,1,0:T(8,128)(2,1)S(1)}, bf16[8,8,8,512]{3,2,1,0:T(8,128)(2,1)S(1)}, u32[]{:S(2)}, u32[]{:S(2)}) collective-permute-start(bf16[8,8,8,512]{3,2,1,0:T(8,128)(2,1)S(1)} %get-tuple-element.522), channel_id=1, source_target_pairs={{0,32},{32,64},{64,96},{96,128},{128,160},{160,192},{192,224},{1,3... | collective-permute-start | bytes 1572872 | tf_op jit(solution)/shard_map/while/body/eval_jaxpr/ppermute | solution.py:29
  91.7 5.8 collective-permute-done.2
  100.2 8.1 %collective-permute-start = (bf16[8,8,4,512]{3,2,1,0:T(4,128)(2,1)S(1)}, bf16[8,8,4,512]{3,2,1,0:T(4,128)(2,1)S(1)}, u32[]{:S(2)}, u32[]{:S(2)}) collective-permute-start(bf16[8,8,4,512]{3,2,1,0:T(4,128)(2,1)S(1)} %get-tuple-element.424), channel_id=1, source_target_pairs={{1,0},{2,1},{3,2},{4,3},{5,4},{6,5},{7,6},{8,7},{9,8},{10,9},{11,1... | collective-permute-start | bytes 786440 | tf_op jit(solution)/shard_map/while/body/eval_jaxpr/ppermute | solution.py:19
  116.7 5.8 collective-permute-done.2
  125.2 7.2 collective-permute-start
  136.4 8.7 %collective-permute-start.2 = (bf16[8,8,8,512]{3,2,1,0:T(8,128)(2,1)S(1)}, bf16[8,8,8,512]{3,2,1,0:T(8,128)(2,1)S(1)}, u32[]{:S(2)}, u32[]{:S(2)}) collective-permute-start(bf16[8,8,8,512]{3,2,1,0:T(8,128)(2,1)S(1)} %get-tuple-element.522), channel_id=1, source_target_pairs={{0,32},{32,64},{64,96},{96,128},{128,160},{160,192},{192,224},{1,3... | collective-permute-start | bytes 1572872 | tf_op jit(solution)/shard_map/while/body/eval_jaxpr/ppermute | solution.py:29
  145.3 5.8 collective-permute-done.2
  153.8 7.4 collective-permute-start
  169.7 5.8 collective-permute-done.2
  178.1 6.8 collective-permute-start
  189.0 8.7 %collective-permute-start.2 = (bf16[8,8,8,512]{3,2,1,0:T(8,128)(2,1)S(1)}, bf16[8,8,8,512]{3,2,1,0:T(8,128)(2,1)S(1)}, u32[]{:S(2)}, u32[]{:S(2)}) collective-permute-start(bf16[8,8,8,512]{3,2,1,0:T(8,128)(2,1)S(1)} %get-tuple-element.522), channel_id=1, source_target_pairs={{0,32},{32,64},{64,96},{96,128},{128,160},{160,192},{192,224},{1,3... | collective-permute-start | bytes 1572872 | tf_op jit(solution)/shard_map/while/body/eval_jaxpr/ppermute | solution.py:29
  197.9 5.8 collective-permute-done.2
  206.4 6.8 collective-permute-start
  221.7 5.8 collective-permute-done.2
  230.1 6.8 collective-permute-start
  241.0 10.7 %collective-permute-start.2 = (bf16[8,8,8,512]{3,2,1,0:T(8,128)(2,1)S(1)}, bf16[8,8,8,512]{3,2,1,0:T(8,128)(2,1)S(1)}, u32[]{:S(2)}, u32[]{:S(2)}) collective-permute-start(bf16[8,8,8,512]{3,2,1,0:T(8,128)(2,1)S(1)} %get-tuple-element.522), channel_id=1, source_target_pairs={{0,32},{32,64},{64,96},{96,128},{128,160},{160,192},{192,224},{1,3... | collective-permute-start | bytes 1572872 | tf_op jit(solution)/shard_map/while/body/eval_jaxpr/ppermute | solution.py:29
  258.8 306.7 %while.28 = (s32[]{:T(128)}, bf16[8,8,8,512]{3,2,1,0:T(8,128)(2,1)}, bf16[2,8,8,8,512]{4,3,2,1,0:T(8,128)(2,1)S(1)}, s32[9]{0:T(128)S(1)}, s32[]{:T(128)}, /*ind...) while((s32[]{:T(128)}, ...), condition=%wide.region_7.8_spmd, body=%wide.region_4.7_spmd.sunk | while | flops 2424045568 | bytes 67764888 | solution.py:138
  262.3 6.7 collective-permute-start.3
  275.7 10.3 %collective-permute-done.5 = bf16[8,8,8,512]{3,2,1,0:T(8,128)(2,1)} collective-permute-done((bf16[8,8,8,512]{3,2,1,0:T(8,128)(2,1)S(1)}, bf16[8,8,8,512]{3,2,1,0:T(8,128)(2,1)}, u32[]{:S(2)}, u32[]{:S(2)}) %collective-permute-start.5) | collective-permute-done | bytes 524320 | tf_op jit(solution)/shard_map/while/body/eval_jaxpr/ppermute | solution.py:29
  289.5 6.8 collective-permute-start.3
  302.9 12.0 %collective-permute-done.5 = bf16[8,8,8,512]{3,2,1,0:T(8,128)(2,1)} collective-permute-done((bf16[8,8,8,512]{3,2,1,0:T(8,128)(2,1)S(1)}, bf16[8,8,8,512]{3,2,1,0:T(8,128)(2,1)}, u32[]{:S(2)}, u32[]{:S(2)}) %collective-permute-start.5) | collective-permute-done | bytes 524320 | tf_op jit(solution)/shard_map/while/body/eval_jaxpr/ppermute | solution.py:29
  318.5 6.8 collective-permute-start.3
  331.9 10.5 %collective-permute-done.5 = bf16[8,8,8,512]{3,2,1,0:T(8,128)(2,1)} collective-permute-done((bf16[8,8,8,512]{3,2,1,0:T(8,128)(2,1)S(1)}, bf16[8,8,8,512]{3,2,1,0:T(8,128)(2,1)}, u32[]{:S(2)}, u32[]{:S(2)}) %collective-permute-start.5) | collective-permute-done | bytes 524320 | tf_op jit(solution)/shard_map/while/body/eval_jaxpr/ppermute | solution.py:29
  345.9 6.8 collective-permute-start.3
  359.3 12.0 %collective-permute-done.5 = bf16[8,8,8,512]{3,2,1,0:T(8,128)(2,1)} collective-permute-done((bf16[8,8,8,512]{3,2,1,0:T(8,128)(2,1)S(1)}, bf16[8,8,8,512]{3,2,1,0:T(8,128)(2,1)}, u32[]{:S(2)}, u32[]{:S(2)}) %collective-permute-start.5) | collective-permute-done | bytes 524320 | tf_op jit(solution)/shard_map/while/body/eval_jaxpr/ppermute | solution.py:29
  374.9 6.8 collective-permute-start.3
  388.3 10.0 %collective-permute-done.5 = bf16[8,8,8,512]{3,2,1,0:T(8,128)(2,1)} collective-permute-done((bf16[8,8,8,512]{3,2,1,0:T(8,128)(2,1)S(1)}, bf16[8,8,8,512]{3,2,1,0:T(8,128)(2,1)}, u32[]{:S(2)}, u32[]{:S(2)}) %collective-permute-start.5) | collective-permute-done | bytes 524320 | tf_op jit(solution)/shard_map/while/body/eval_jaxpr/ppermute | solution.py:29
  401.8 6.8 collective-permute-start.3
  415.2 12.5 %collective-permute-done.5 = bf16[8,8,8,512]{3,2,1,0:T(8,128)(2,1)} collective-permute-done((bf16[8,8,8,512]{3,2,1,0:T(8,128)(2,1)S(1)}, bf16[8,8,8,512]{3,2,1,0:T(8,128)(2,1)}, u32[]{:S(2)}, u32[]{:S(2)}) %collective-permute-start.5) | collective-permute-done | bytes 524320 | tf_op jit(solution)/shard_map/while/body/eval_jaxpr/ppermute | solution.py:29
  431.3 6.8 collective-permute-start.3
  444.6 54.9 %collective-permute-done.5 = bf16[8,8,8,512]{3,2,1,0:T(8,128)(2,1)} collective-permute-done((bf16[8,8,8,512]{3,2,1,0:T(8,128)(2,1)S(1)}, bf16[8,8,8,512]{3,2,1,0:T(8,128)(2,1)}, u32[]{:S(2)}, u32[]{:S(2)}) %collective-permute-start.5) | collective-permute-done | bytes 524320 | tf_op jit(solution)/shard_map/while/body/eval_jaxpr/ppermute | solution.py:29
  503.1 6.8 collective-permute-start.3
  514.9 6.8 conditional.5
  523.3 10.0 %collective-permute-done.5 = bf16[8,8,8,512]{3,2,1,0:T(8,128)(2,1)} collective-permute-done((bf16[8,8,8,512]{3,2,1,0:T(8,128)(2,1)S(1)}, bf16[8,8,8,512]{3,2,1,0:T(8,128)(2,1)}, u32[]{:S(2)}, u32[]{:S(2)}) %collective-permute-start.5) | collective-permute-done | bytes 524320 | tf_op jit(solution)/shard_map/while/body/eval_jaxpr/ppermute | solution.py:29
  536.8 6.8 collective-permute-start.3
  548.6 6.8 conditional.5
  557.0 8.5 %collective-permute-done.5 = bf16[8,8,8,512]{3,2,1,0:T(8,128)(2,1)} collective-permute-done((bf16[8,8,8,512]{3,2,1,0:T(8,128)(2,1)S(1)}, bf16[8,8,8,512]{3,2,1,0:T(8,128)(2,1)}, u32[]{:S(2)}, u32[]{:S(2)}) %collective-permute-start.5) | collective-permute-done | bytes 524320 | tf_op jit(solution)/shard_map/while/body/eval_jaxpr/ppermute | solution.py:29
  567.7 67.9 %all-reduce.4.cloned.1.call-done = bf16[16,8,8,512]{3,2,0,1:T(8,128)(2,1)} async-done(((bf16[16,8,8,512]{3,2,0,1:T(8,128)(2,1)}), bf16[16,8,8,512]{3,2,0,1:T(8,128)(2,1)}) %all-reduce.4.cloned.1.call-update) | async-done | bytes 1048592 | tf_op jit(solution)/shard_map/psum | solution.py:34
  637.3 68.1 %psum.29 = f32[16,16]{1,0:T(8,128)S(1)} all-reduce(f32[16,16]{1,0:T(8,128)S(1)} %convolution_multiply_fusion.1), channel_id=1, replica_groups=mesh['section'=8,'lon'=32] {'lon'}, use_global_device_ids=true, to_apply=%region_9.10 | all-reduce | flops 256 | bytes 2048 | tf_op jit(solution)/shard_map/psum | solution.py:159
  705.4 13.1 %psum.30 = f32[16,16]{1,0:T(8,128)S(1)} all-reduce(f32[16,16]{1,0:T(8,128)S(1)} %psum.29), channel_id=1, replica_groups=mesh['section'=8,'lon'=32] {'section'}, use_global_device_ids=true, to_apply=%region_10.11 | all-reduce | flops 256 | bytes 2048 | tf_op jit(solution)/shard_map/psum | solution.py:160
  720.1 74.7 %psum.31 = f32[16,16]{1,0:T(8,128)} all-reduce(f32[16,16]{1,0:T(8,128)S(1)} %convolution_multiply_fusion), channel_id=1, replica_groups=mesh['section'=8,'lon'=32] {'section','lon'}, use_global_device_ids=true, to_apply=%region_11.12 | all-reduce | flops 256 | bytes 2048 | tf_op jit(solution)/shard_map/psum | solution.py:163
  (287 shorter events, 203.1 us)
Async XLA Ops:
  7.2 628.4 %all-reduce.4.cloned.1.call-start = ((), (), s32[]{:S(2)}) async-start(), calls=%async_computation | async-start | bytes 2097152 | tf_op jit(solution)/shard_map/psum | solution.py:34
  10.9 6.7 collective-permute-start
  14.2 4.0 collective-permute-start.1
  25.4 7.4 collective-permute-start.2
  35.4 11.0 %collective-permute-start = (bf16[8,8,4,512]{3,2,1,0:T(4,128)(2,1)S(1)}, bf16[8,8,4,512]{3,2,1,0:T(4,128)(2,1)S(1)}, u32[]{:S(2)}, u32[]{:S(2)}) collective-permute-start(bf16[8,8,4,512]{3,2,1,0:T(4,128)(2,1)S(1)} %get-tuple-element.424), channel_id=1, source_target_pairs={{1,0},{2,1},{3,2},{4,3},{5,4},{6,5},{7,6},{8,7},{9,8},{10,9},{11,1... | collective-permute-start | bytes 786440 | tf_op jit(solution)/shard_map/while/body/eval_jaxpr/ppermute | solution.py:19
  44.1 3.9 collective-permute-start.1
  55.2 9.9 %collective-permute-start.2 = (bf16[8,8,8,512]{3,2,1,0:T(8,128)(2,1)S(1)}, bf16[8,8,8,512]{3,2,1,0:T(8,128)(2,1)S(1)}, u32[]{:S(2)}, u32[]{:S(2)}) collective-permute-start(bf16[8,8,8,512]{3,2,1,0:T(8,128)(2,1)S(1)} %get-tuple-element.522), channel_id=1, source_target_pairs={{0,32},{32,64},{64,96},{96,128},{128,160},{160,192},{192,224},{1,3... | collective-permute-start | bytes 1572872 | tf_op jit(solution)/shard_map/while/body/eval_jaxpr/ppermute | solution.py:29
  67.8 10.2 %collective-permute-start = (bf16[8,8,4,512]{3,2,1,0:T(4,128)(2,1)S(1)}, bf16[8,8,4,512]{3,2,1,0:T(4,128)(2,1)S(1)}, u32[]{:S(2)}, u32[]{:S(2)}) collective-permute-start(bf16[8,8,4,512]{3,2,1,0:T(4,128)(2,1)S(1)} %get-tuple-element.424), channel_id=1, source_target_pairs={{1,0},{2,1},{3,2},{4,3},{5,4},{6,5},{7,6},{8,7},{9,8},{10,9},{11,1... | collective-permute-start | bytes 786440 | tf_op jit(solution)/shard_map/while/body/eval_jaxpr/ppermute | solution.py:19
  76.8 3.3 collective-permute-start.1
  80.9 16.7 %collective-permute-start.2 = (bf16[8,8,8,512]{3,2,1,0:T(8,128)(2,1)S(1)}, bf16[8,8,8,512]{3,2,1,0:T(8,128)(2,1)S(1)}, u32[]{:S(2)}, u32[]{:S(2)}) collective-permute-start(bf16[8,8,8,512]{3,2,1,0:T(8,128)(2,1)S(1)} %get-tuple-element.522), channel_id=1, source_target_pairs={{0,32},{32,64},{64,96},{96,128},{128,160},{160,192},{192,224},{1,3... | collective-permute-start | bytes 1572872 | tf_op jit(solution)/shard_map/while/body/eval_jaxpr/ppermute | solution.py:29
  100.2 9.3 %collective-permute-start = (bf16[8,8,4,512]{3,2,1,0:T(4,128)(2,1)S(1)}, bf16[8,8,4,512]{3,2,1,0:T(4,128)(2,1)S(1)}, u32[]{:S(2)}, u32[]{:S(2)}) collective-permute-start(bf16[8,8,4,512]{3,2,1,0:T(4,128)(2,1)S(1)} %get-tuple-element.424), channel_id=1, source_target_pairs={{1,0},{2,1},{3,2},{4,3},{5,4},{6,5},{7,6},{8,7},{9,8},{10,9},{11,1... | collective-permute-start | bytes 786440 | tf_op jit(solution)/shard_map/while/body/eval_jaxpr/ppermute | solution.py:19
  108.3 3.3 collective-permute-start.1
  112.3 10.2 %collective-permute-start.2 = (bf16[8,8,8,512]{3,2,1,0:T(8,128)(2,1)S(1)}, bf16[8,8,8,512]{3,2,1,0:T(8,128)(2,1)S(1)}, u32[]{:S(2)}, u32[]{:S(2)}) collective-permute-start(bf16[8,8,8,512]{3,2,1,0:T(8,128)(2,1)S(1)} %get-tuple-element.522), channel_id=1, source_target_pairs={{0,32},{32,64},{64,96},{96,128},{128,160},{160,192},{192,224},{1,3... | collective-permute-start | bytes 1572872 | tf_op jit(solution)/shard_map/while/body/eval_jaxpr/ppermute | solution.py:29
  125.2 8.3 %collective-permute-start = (bf16[8,8,4,512]{3,2,1,0:T(4,128)(2,1)S(1)}, bf16[8,8,4,512]{3,2,1,0:T(4,128)(2,1)S(1)}, u32[]{:S(2)}, u32[]{:S(2)}) collective-permute-start(bf16[8,8,4,512]{3,2,1,0:T(4,128)(2,1)S(1)} %get-tuple-element.424), channel_id=1, source_target_pairs={{1,0},{2,1},{3,2},{4,3},{5,4},{6,5},{7,6},{8,7},{9,8},{10,9},{11,1... | collective-permute-start | bytes 786440 | tf_op jit(solution)/shard_map/while/body/eval_jaxpr/ppermute | solution.py:19
  132.3 3.3 collective-permute-start.1
  136.4 14.8 %collective-permute-start.2 = (bf16[8,8,8,512]{3,2,1,0:T(8,128)(2,1)S(1)}, bf16[8,8,8,512]{3,2,1,0:T(8,128)(2,1)S(1)}, u32[]{:S(2)}, u32[]{:S(2)}) collective-permute-start(bf16[8,8,8,512]{3,2,1,0:T(8,128)(2,1)S(1)} %get-tuple-element.522), channel_id=1, source_target_pairs={{0,32},{32,64},{64,96},{96,128},{128,160},{160,192},{192,224},{1,3... | collective-permute-start | bytes 1572872 | tf_op jit(solution)/shard_map/while/body/eval_jaxpr/ppermute | solution.py:29
  153.8 8.6 %collective-permute-start = (bf16[8,8,4,512]{3,2,1,0:T(4,128)(2,1)S(1)}, bf16[8,8,4,512]{3,2,1,0:T(4,128)(2,1)S(1)}, u32[]{:S(2)}, u32[]{:S(2)}) collective-permute-start(bf16[8,8,4,512]{3,2,1,0:T(4,128)(2,1)S(1)} %get-tuple-element.424), channel_id=1, source_target_pairs={{1,0},{2,1},{3,2},{4,3},{5,4},{6,5},{7,6},{8,7},{9,8},{10,9},{11,1... | collective-permute-start | bytes 786440 | tf_op jit(solution)/shard_map/while/body/eval_jaxpr/ppermute | solution.py:19
  161.2 3.3 collective-permute-start.1
  165.3 10.2 %collective-permute-start.2 = (bf16[8,8,8,512]{3,2,1,0:T(8,128)(2,1)S(1)}, bf16[8,8,8,512]{3,2,1,0:T(8,128)(2,1)S(1)}, u32[]{:S(2)}, u32[]{:S(2)}) collective-permute-start(bf16[8,8,8,512]{3,2,1,0:T(8,128)(2,1)S(1)} %get-tuple-element.522), channel_id=1, source_target_pairs={{0,32},{32,64},{64,96},{96,128},{128,160},{160,192},{192,224},{1,3... | collective-permute-start | bytes 1572872 | tf_op jit(solution)/shard_map/while/body/eval_jaxpr/ppermute | solution.py:29
  178.1 8.0 collective-permute-start
  184.9 3.3 collective-permute-start.1
  189.0 14.8 %collective-permute-start.2 = (bf16[8,8,8,512]{3,2,1,0:T(8,128)(2,1)S(1)}, bf16[8,8,8,512]{3,2,1,0:T(8,128)(2,1)S(1)}, u32[]{:S(2)}, u32[]{:S(2)}) collective-permute-start(bf16[8,8,8,512]{3,2,1,0:T(8,128)(2,1)S(1)} %get-tuple-element.522), channel_id=1, source_target_pairs={{0,32},{32,64},{64,96},{96,128},{128,160},{160,192},{192,224},{1,3... | collective-permute-start | bytes 1572872 | tf_op jit(solution)/shard_map/while/body/eval_jaxpr/ppermute | solution.py:29
  206.4 8.0 collective-permute-start
  213.2 3.3 collective-permute-start.1
  217.3 10.2 %collective-permute-start.2 = (bf16[8,8,8,512]{3,2,1,0:T(8,128)(2,1)S(1)}, bf16[8,8,8,512]{3,2,1,0:T(8,128)(2,1)S(1)}, u32[]{:S(2)}, u32[]{:S(2)}) collective-permute-start(bf16[8,8,8,512]{3,2,1,0:T(8,128)(2,1)S(1)} %get-tuple-element.522), channel_id=1, source_target_pairs={{0,32},{32,64},{64,96},{96,128},{128,160},{160,192},{192,224},{1,3... | collective-permute-start | bytes 1572872 | tf_op jit(solution)/shard_map/while/body/eval_jaxpr/ppermute | solution.py:29
  230.1 8.0 collective-permute-start
  236.9 3.3 collective-permute-start.1
  241.0 16.8 %collective-permute-start.2 = (bf16[8,8,8,512]{3,2,1,0:T(8,128)(2,1)S(1)}, bf16[8,8,8,512]{3,2,1,0:T(8,128)(2,1)S(1)}, u32[]{:S(2)}, u32[]{:S(2)}) collective-permute-start(bf16[8,8,8,512]{3,2,1,0:T(8,128)(2,1)S(1)} %get-tuple-element.522), channel_id=1, source_target_pairs={{0,32},{32,64},{64,96},{96,128},{128,160},{160,192},{192,224},{1,3... | collective-permute-start | bytes 1572872 | tf_op jit(solution)/shard_map/while/body/eval_jaxpr/ppermute | solution.py:29
  262.3 8.2 %collective-permute-start.3 = (bf16[8,8,4,512]{3,2,1,0:T(4,128)(2,1)}, bf16[8,8,4,512]{3,2,1,0:T(4,128)(2,1)}, u32[]{:S(2)}, u32[]{:S(2)}) collective-permute-start(bf16[8,8,4,512]{3,2,1,0:T(4,128)(2,1)} %get-tuple-element.439), channel_id=1, source_target_pairs={{1,0},{2,1},{3,2},{4,3},{5,4},{6,5},{7,6},{8,7},{9,8},{10,9},{11,1... | collective-permute-start | bytes 786440 | tf_op jit(solution)/shard_map/while/body/eval_jaxpr/ppermute | solution.py:19
  269.1 3.3 collective-permute-start.4
  274.2 11.8 %collective-permute-start.5 = (bf16[8,8,8,512]{3,2,1,0:T(8,128)(2,1)S(1)}, bf16[8,8,8,512]{3,2,1,0:T(8,128)(2,1)}, u32[]{:S(2)}, u32[]{:S(2)}) collective-permute-start(bf16[8,8,8,512]{3,2,1,0:T(8,128)(2,1)S(1)} %get-tuple-element.523), channel_id=1, source_target_pairs={{32,0},{64,32},{96,64},{128,96},{160,128},{192,160},{224,192},{33,... | collective-permute-start | bytes 1572872 | tf_op jit(solution)/shard_map/while/body/eval_jaxpr/ppermute | solution.py:29
  289.5 8.3 %collective-permute-start.3 = (bf16[8,8,4,512]{3,2,1,0:T(4,128)(2,1)}, bf16[8,8,4,512]{3,2,1,0:T(4,128)(2,1)}, u32[]{:S(2)}, u32[]{:S(2)}) collective-permute-start(bf16[8,8,4,512]{3,2,1,0:T(4,128)(2,1)} %get-tuple-element.439), channel_id=1, source_target_pairs={{1,0},{2,1},{3,2},{4,3},{5,4},{6,5},{7,6},{8,7},{9,8},{10,9},{11,1... | collective-permute-start | bytes 786440 | tf_op jit(solution)/shard_map/while/body/eval_jaxpr/ppermute | solution.py:19
  296.3 3.3 collective-permute-start.4
  301.4 13.6 %collective-permute-start.5 = (bf16[8,8,8,512]{3,2,1,0:T(8,128)(2,1)S(1)}, bf16[8,8,8,512]{3,2,1,0:T(8,128)(2,1)}, u32[]{:S(2)}, u32[]{:S(2)}) collective-permute-start(bf16[8,8,8,512]{3,2,1,0:T(8,128)(2,1)S(1)} %get-tuple-element.523), channel_id=1, source_target_pairs={{32,0},{64,32},{96,64},{128,96},{160,128},{192,160},{224,192},{33,... | collective-permute-start | bytes 1572872 | tf_op jit(solution)/shard_map/while/body/eval_jaxpr/ppermute | solution.py:29
  318.5 8.3 %collective-permute-start.3 = (bf16[8,8,4,512]{3,2,1,0:T(4,128)(2,1)}, bf16[8,8,4,512]{3,2,1,0:T(4,128)(2,1)}, u32[]{:S(2)}, u32[]{:S(2)}) collective-permute-start(bf16[8,8,4,512]{3,2,1,0:T(4,128)(2,1)} %get-tuple-element.439), channel_id=1, source_target_pairs={{1,0},{2,1},{3,2},{4,3},{5,4},{6,5},{7,6},{8,7},{9,8},{10,9},{11,1... | collective-permute-start | bytes 786440 | tf_op jit(solution)/shard_map/while/body/eval_jaxpr/ppermute | solution.py:19
  330.3 12.0 %collective-permute-start.5 = (bf16[8,8,8,512]{3,2,1,0:T(8,128)(2,1)S(1)}, bf16[8,8,8,512]{3,2,1,0:T(8,128)(2,1)}, u32[]{:S(2)}, u32[]{:S(2)}) collective-permute-start(bf16[8,8,8,512]{3,2,1,0:T(8,128)(2,1)S(1)} %get-tuple-element.523), channel_id=1, source_target_pairs={{32,0},{64,32},{96,64},{128,96},{160,128},{192,160},{224,192},{33,... | collective-permute-start | bytes 1572872 | tf_op jit(solution)/shard_map/while/body/eval_jaxpr/ppermute | solution.py:29
  345.9 8.3 %collective-permute-start.3 = (bf16[8,8,4,512]{3,2,1,0:T(4,128)(2,1)}, bf16[8,8,4,512]{3,2,1,0:T(4,128)(2,1)}, u32[]{:S(2)}, u32[]{:S(2)}) collective-permute-start(bf16[8,8,4,512]{3,2,1,0:T(4,128)(2,1)} %get-tuple-element.439), channel_id=1, source_target_pairs={{1,0},{2,1},{3,2},{4,3},{5,4},{6,5},{7,6},{8,7},{9,8},{10,9},{11,1... | collective-permute-start | bytes 786440 | tf_op jit(solution)/shard_map/while/body/eval_jaxpr/ppermute | solution.py:19
  357.8 13.6 %collective-permute-start.5 = (bf16[8,8,8,512]{3,2,1,0:T(8,128)(2,1)S(1)}, bf16[8,8,8,512]{3,2,1,0:T(8,128)(2,1)}, u32[]{:S(2)}, u32[]{:S(2)}) collective-permute-start(bf16[8,8,8,512]{3,2,1,0:T(8,128)(2,1)S(1)} %get-tuple-element.523), channel_id=1, source_target_pairs={{32,0},{64,32},{96,64},{128,96},{160,128},{192,160},{224,192},{33,... | collective-permute-start | bytes 1572872 | tf_op jit(solution)/shard_map/while/body/eval_jaxpr/ppermute | solution.py:29
  374.9 8.3 %collective-permute-start.3 = (bf16[8,8,4,512]{3,2,1,0:T(4,128)(2,1)}, bf16[8,8,4,512]{3,2,1,0:T(4,128)(2,1)}, u32[]{:S(2)}, u32[]{:S(2)}) collective-permute-start(bf16[8,8,4,512]{3,2,1,0:T(4,128)(2,1)} %get-tuple-element.439), channel_id=1, source_target_pairs={{1,0},{2,1},{3,2},{4,3},{5,4},{6,5},{7,6},{8,7},{9,8},{10,9},{11,1... | collective-permute-start | bytes 786440 | tf_op jit(solution)/shard_map/while/body/eval_jaxpr/ppermute | solution.py:19
  386.7 11.5 %collective-permute-start.5 = (bf16[8,8,8,512]{3,2,1,0:T(8,128)(2,1)S(1)}, bf16[8,8,8,512]{3,2,1,0:T(8,128)(2,1)}, u32[]{:S(2)}, u32[]{:S(2)}) collective-permute-start(bf16[8,8,8,512]{3,2,1,0:T(8,128)(2,1)S(1)} %get-tuple-element.523), channel_id=1, source_target_pairs={{32,0},{64,32},{96,64},{128,96},{160,128},{192,160},{224,192},{33,... | collective-permute-start | bytes 1572872 | tf_op jit(solution)/shard_map/while/body/eval_jaxpr/ppermute | solution.py:29
  401.8 8.3 %collective-permute-start.3 = (bf16[8,8,4,512]{3,2,1,0:T(4,128)(2,1)}, bf16[8,8,4,512]{3,2,1,0:T(4,128)(2,1)}, u32[]{:S(2)}, u32[]{:S(2)}) collective-permute-start(bf16[8,8,4,512]{3,2,1,0:T(4,128)(2,1)} %get-tuple-element.439), channel_id=1, source_target_pairs={{1,0},{2,1},{3,2},{4,3},{5,4},{6,5},{7,6},{8,7},{9,8},{10,9},{11,1... | collective-permute-start | bytes 786440 | tf_op jit(solution)/shard_map/while/body/eval_jaxpr/ppermute | solution.py:19
  413.7 14.0 %collective-permute-start.5 = (bf16[8,8,8,512]{3,2,1,0:T(8,128)(2,1)S(1)}, bf16[8,8,8,512]{3,2,1,0:T(8,128)(2,1)}, u32[]{:S(2)}, u32[]{:S(2)}) collective-permute-start(bf16[8,8,8,512]{3,2,1,0:T(8,128)(2,1)S(1)} %get-tuple-element.523), channel_id=1, source_target_pairs={{32,0},{64,32},{96,64},{128,96},{160,128},{192,160},{224,192},{33,... | collective-permute-start | bytes 1572872 | tf_op jit(solution)/shard_map/while/body/eval_jaxpr/ppermute | solution.py:29
  431.3 8.3 %collective-permute-start.3 = (bf16[8,8,4,512]{3,2,1,0:T(4,128)(2,1)}, bf16[8,8,4,512]{3,2,1,0:T(4,128)(2,1)}, u32[]{:S(2)}, u32[]{:S(2)}) collective-permute-start(bf16[8,8,4,512]{3,2,1,0:T(4,128)(2,1)} %get-tuple-element.439), channel_id=1, source_target_pairs={{1,0},{2,1},{3,2},{4,3},{5,4},{6,5},{7,6},{8,7},{9,8},{10,9},{11,1... | collective-permute-start | bytes 786440 | tf_op jit(solution)/shard_map/while/body/eval_jaxpr/ppermute | solution.py:19
  443.1 56.5 %collective-permute-start.5 = (bf16[8,8,8,512]{3,2,1,0:T(8,128)(2,1)S(1)}, bf16[8,8,8,512]{3,2,1,0:T(8,128)(2,1)}, u32[]{:S(2)}, u32[]{:S(2)}) collective-permute-start(bf16[8,8,8,512]{3,2,1,0:T(8,128)(2,1)S(1)} %get-tuple-element.523), channel_id=1, source_target_pairs={{32,0},{64,32},{96,64},{128,96},{160,128},{192,160},{224,192},{33,... | collective-permute-start | bytes 1572872 | tf_op jit(solution)/shard_map/while/body/eval_jaxpr/ppermute | solution.py:29
  503.1 8.3 %collective-permute-start.3 = (bf16[8,8,4,512]{3,2,1,0:T(4,128)(2,1)}, bf16[8,8,4,512]{3,2,1,0:T(4,128)(2,1)}, u32[]{:S(2)}, u32[]{:S(2)}) collective-permute-start(bf16[8,8,4,512]{3,2,1,0:T(4,128)(2,1)} %get-tuple-element.439), channel_id=1, source_target_pairs={{1,0},{2,1},{3,2},{4,3},{5,4},{6,5},{7,6},{8,7},{9,8},{10,9},{11,1... | collective-permute-start | bytes 786440 | tf_op jit(solution)/shard_map/while/body/eval_jaxpr/ppermute | solution.py:19
  521.8 11.5 %collective-permute-start.5 = (bf16[8,8,8,512]{3,2,1,0:T(8,128)(2,1)S(1)}, bf16[8,8,8,512]{3,2,1,0:T(8,128)(2,1)}, u32[]{:S(2)}, u32[]{:S(2)}) collective-permute-start(bf16[8,8,8,512]{3,2,1,0:T(8,128)(2,1)S(1)} %get-tuple-element.523), channel_id=1, source_target_pairs={{32,0},{64,32},{96,64},{128,96},{160,128},{192,160},{224,192},{33,... | collective-permute-start | bytes 1572872 | tf_op jit(solution)/shard_map/while/body/eval_jaxpr/ppermute | solution.py:29
  536.8 8.3 %collective-permute-start.3 = (bf16[8,8,4,512]{3,2,1,0:T(4,128)(2,1)}, bf16[8,8,4,512]{3,2,1,0:T(4,128)(2,1)}, u32[]{:S(2)}, u32[]{:S(2)}) collective-permute-start(bf16[8,8,4,512]{3,2,1,0:T(4,128)(2,1)} %get-tuple-element.439), channel_id=1, source_target_pairs={{1,0},{2,1},{3,2},{4,3},{5,4},{6,5},{7,6},{8,7},{9,8},{10,9},{11,1... | collective-permute-start | bytes 786440 | tf_op jit(solution)/shard_map/while/body/eval_jaxpr/ppermute | solution.py:19
  555.5 10.0 %collective-permute-start.5 = (bf16[8,8,8,512]{3,2,1,0:T(8,128)(2,1)S(1)}, bf16[8,8,8,512]{3,2,1,0:T(8,128)(2,1)}, u32[]{:S(2)}, u32[]{:S(2)}) collective-permute-start(bf16[8,8,8,512]{3,2,1,0:T(8,128)(2,1)S(1)} %get-tuple-element.523), channel_id=1, source_target_pairs={{32,0},{64,32},{96,64},{128,96},{160,128},{192,160},{224,192},{33,... | collective-permute-start | bytes 1572872 | tf_op jit(solution)/shard_map/while/body/eval_jaxpr/ppermute | solution.py:29
  (15 other events, 990.3 us)
Sparse Core Ops, SparseCore 0:
  566.8 68.7 all-reduce.3
